TPU v7x, 32 devices: a whole 2x2x4 slice. The times are simulated.
32 devices in a mesh: fsdp: 4 (over x, core), seq: 8 (over z, y).
Axes of the slice: x: 2, y: 2, z: 4, core: 2. Of those that a mesh axis runs over, the one named last changes fastest.
Arguments:
- tokens: bfloat16 [4, 56, 28, 512], P('fsdp', 'seq'), may hold values from -6 to 6
- cotangent: bfloat16 [4, 56, 28, 512], P('fsdp', 'seq'), may hold values from -6 to 6
- region_ids: int32 [56, 28], replicated, may hold values from 0 to 3
- relative_index: int32 [49, 49], replicated, may hold values from 0 to 168, as said below
- first_gain: bfloat16 [512], P('fsdp'), may hold values from 0.5 to 1.5
- first_offset: bfloat16 [512], P('fsdp'), may hold values from -3 to 3
- qkv_weight: bfloat16 [512, 1536], P('fsdp'), may hold values from -0.25 to 0.25
- proj_weight: bfloat16 [512, 512], P('fsdp'), may hold values from -0.75 to 0.75
- bias_table: bfloat16 [16, 169], P('fsdp'), may hold values from -4 to 4
- second_gain: bfloat16 [512], P('fsdp'), may hold values from 0.5 to 1.5
- second_offset: bfloat16 [512], P('fsdp'), may hold values from -3 to 3
- expand_weight: bfloat16 [512, 2048], P('fsdp'), may hold values from -0.25 to 0.25
- reduce_weight: bfloat16 [2048, 512], P('fsdp'), may hold values from -0.125 to 0.125
Outputs:
- output: bfloat16 [4, 56, 28, 512], P('fsdp', 'seq')
- tokens_grad: float32 [4, 56, 28, 512], P('fsdp', 'seq')
- first_gain_grad: float32 [512], P('fsdp')
- first_offset_grad: float32 [512], P('fsdp')
- qkv_weight_grad: float32 [512, 1536], P('fsdp')
- proj_weight_grad: float32 [512, 512], P('fsdp')
- bias_table_grad: float32 [16, 169], P('fsdp')
- second_gain_grad: float32 [512], P('fsdp')
- second_offset_grad: float32 [512], P('fsdp')
- expand_weight_grad: float32 [512, 2048], P('fsdp')
- reduce_weight_grad: float32 [2048, 512], P('fsdp')
Inputs may be any that keep to these rules, and one draw needn't show every extreme that they name: relative_index[i, j] depends only on the row and column offsets between positions i and j of a 7 x 7 window, and distinct offsets give distinct entries.
All inputs are finite; a program needn't handle non-finite values.
Results may differ from a plain program's by a relative error of at most 0.018.
Values may be sent and summed in bfloat16 or wider, within the bound.
A program may use at most 128 MiB of HBM per device.

v0:
```python
import jax
import jax.numpy as jnp
from jax import lax
from jax.sharding import PartitionSpec as P

WS = 7
SHIFT = 3
EPSILON = 1e-05
MASKED = -100.0
SQRT_HALF = 0.7071067811865476
INV_ROOT_TAU = 0.3989422804014327


def layer_norm(values, norm_gain, norm_offset):
    average = jnp.mean(values, axis=-1, keepdims=True)
    centred = values - average
    variance = jnp.mean(centred * centred, axis=-1, keepdims=True)
    inverse = lax.rsqrt(variance + EPSILON)
    normed = centred * inverse
    return (normed * norm_gain + norm_offset, normed, inverse)


def norm_back(upstream, normed, inverse, norm_gain):
    scaled = upstream * norm_gain
    mean_grad = jnp.mean(scaled, axis=-1, keepdims=True)
    second = jnp.mean(scaled * normed, axis=-1, keepdims=True)
    grad_in = inverse * (scaled - mean_grad - normed * second)
    lead_axes = tuple(range(upstream.ndim - 1))
    return (grad_in, jnp.sum(upstream * normed, axis=lead_axes), jnp.sum(upstream, axis=lead_axes))


def gelu_parts(hidden):
    normal_cdf = 0.5 * (1.0 + jax.scipy.special.erf(hidden * SQRT_HALF))
    density = jnp.exp(-0.5 * hidden * hidden) * INV_ROOT_TAU
    return (hidden * normal_cdf, normal_cdf + hidden * density)


def to_windows(field_in, num_heads):
    lead_dims = field_in.shape[:-3]
    num_rows, num_cols, features = field_in.shape[-3:]
    lead_count = len(lead_dims)
    pieces = field_in.reshape(
        lead_dims + (num_rows // WS, WS, num_cols // WS, WS, num_heads, features // num_heads)
    )
    axis_order = tuple(range(lead_count)) + (
        lead_count,
        lead_count + 2,
        lead_count + 4,
        lead_count + 1,
        lead_count + 3,
        lead_count + 5,
    )
    return pieces.transpose(axis_order).reshape(
        lead_dims + (num_rows // WS, num_cols // WS, num_heads, WS * WS, features // num_heads)
    )


def from_windows(window_tiles):
    lead_dims = window_tiles.shape[:-5]
    win_rows, win_cols, num_heads, positions, head_dim = window_tiles.shape[-5:]
    lead_count = len(lead_dims)
    pieces = window_tiles.reshape(lead_dims + (win_rows, win_cols, num_heads, WS, WS, head_dim))
    axis_order = tuple(range(lead_count)) + (
        lead_count,
        lead_count + 3,
        lead_count + 1,
        lead_count + 4,
        lead_count + 2,
        lead_count + 5,
    )
    return pieces.transpose(axis_order).reshape(
        lead_dims + (win_rows * WS, win_cols * WS, num_heads * head_dim)
    )


def make_mask(regions):
    num_rows, num_cols = regions.shape
    region_tiles = (
        regions.reshape(num_rows // WS, WS, num_cols // WS, WS)
        .transpose(0, 2, 1, 3)
        .reshape(num_rows // WS, num_cols // WS, WS * WS)
    )
    same_region = region_tiles[..., :, None] == region_tiles[..., None, :]
    return jnp.where(same_region, 0.0, MASKED).astype(jnp.float32)


def one_hot_index(relative_index, entries):
    return (relative_index[..., None] == jnp.arange(entries, dtype=jnp.int32)).astype(jnp.float32)


def table_bias(table_rows, relative_index):
    onehot = one_hot_index(relative_index, table_rows.shape[-1])
    return jnp.einsum("ijr,hr->hij", onehot, table_rows, precision=lax.Precision.HIGHEST)


def table_grad(bias_grad, relative_index, entries):
    onehot = one_hot_index(relative_index, entries)
    return jnp.einsum("hij,ijr->hr", bias_grad, onehot, precision=lax.Precision.HIGHEST)


def attend_forward(qkv_field, rel_bias, mask_add, num_heads):
    rolled = jnp.roll(qkv_field, -SHIFT, axis=-2)
    window_tiles = to_windows(rolled, num_heads)
    queries, key_tiles, value_tiles = (window_tiles[:, 0], window_tiles[:, 1], window_tiles[:, 2])
    scores = (
        jnp.einsum("bxyhid,bxyhjd->bxyhij", queries, key_tiles, preferred_element_type=jnp.float32)
        + rel_bias
        + mask_add[:, :, None]
    )
    exp_scores = jnp.exp(scores)
    row_total = jnp.sum(exp_scores, axis=-1, keepdims=True)
    attn_probs = (exp_scores / row_total).astype(jnp.bfloat16)
    attn_tiles = jnp.einsum(
        "bxyhij,bxyhjd->bxyhid", attn_probs, value_tiles, preferred_element_type=jnp.float32
    ).astype(jnp.bfloat16)
    field_out = jnp.roll(from_windows(attn_tiles), SHIFT, axis=-2)
    return (field_out, (queries, key_tiles, value_tiles, jnp.log(row_total)))


def attend_backward(grad_field, kept_state, rel_bias, mask_add, num_heads):
    queries, key_tiles, value_tiles, log_total = kept_state
    grad_tiles = to_windows(jnp.roll(grad_field, -SHIFT, axis=-2), num_heads)
    scores = (
        jnp.einsum("bxyhid,bxyhjd->bxyhij", queries, key_tiles, preferred_element_type=jnp.float32)
        + rel_bias
        + mask_add[:, :, None]
    )
    probs_back = jnp.exp(scores - log_total)
    value_grad = jnp.einsum(
        "bxyhij,bxyhid->bxyhjd",
        probs_back.astype(jnp.bfloat16),
        grad_tiles,
        preferred_element_type=jnp.float32,
    )
    prob_grad = jnp.einsum(
        "bxyhid,bxyhjd->bxyhij", grad_tiles, value_tiles, preferred_element_type=jnp.float32
    )
    score_grad = probs_back * (prob_grad - jnp.sum(probs_back * prob_grad, axis=-1, keepdims=True))
    score_low = score_grad.astype(jnp.bfloat16)
    query_scale = queries.shape[-1] ** (-0.5)
    query_grad = (
        jnp.einsum(
            "bxyhij,bxyhjd->bxyhid", score_low, key_tiles, preferred_element_type=jnp.float32
        )
        * query_scale
    )
    key_grad = jnp.einsum(
        "bxyhij,bxyhid->bxyhjd", score_low, queries, preferred_element_type=jnp.float32
    )
    stacked = jnp.stack([query_grad, key_grad, value_grad], axis=1).astype(jnp.bfloat16)
    field_grad = jnp.roll(from_windows(stacked), SHIFT, axis=-2)
    return (field_grad, jnp.sum(score_grad, axis=(0, 1, 2)))


def shards(
    tokens,
    cotangent,
    region_ids,
    relative_index,
    first_gain,
    first_offset,
    qkv_weight,
    proj_weight,
    bias_table,
    second_gain,
    second_offset,
    expand_weight,
    reduce_weight,
):
    gathered = (
        lax.all_gather(first_gain, "fsdp", axis=0, tiled=True),
        lax.all_gather(first_offset, "fsdp", axis=0, tiled=True),
        lax.all_gather(qkv_weight, "fsdp", axis=0, tiled=True),
        lax.all_gather(proj_weight, "fsdp", axis=0, tiled=True),
        lax.all_gather(bias_table, "fsdp", axis=0, tiled=True),
        lax.all_gather(second_gain, "fsdp", axis=0, tiled=True),
        lax.all_gather(second_offset, "fsdp", axis=0, tiled=True),
        lax.all_gather(expand_weight, "fsdp", axis=0, tiled=True),
        lax.all_gather(reduce_weight, "fsdp", axis=0, tiled=True),
    )
    gain_one = gathered[0].astype(jnp.float32)
    offset_one = gathered[1].astype(jnp.float32)
    qkv_full = gathered[2]
    proj_full = gathered[3]
    table_full = gathered[4].astype(jnp.float32)
    gain_two = gathered[5].astype(jnp.float32)
    offset_two = gathered[6].astype(jnp.float32)
    expand_full = gathered[7]
    reduce_full = gathered[8]
    num_images, num_rows, num_cols, width = tokens.shape
    num_heads, entries = table_full.shape
    query_scale = (width // num_heads) ** (-0.5)
    factors = jnp.array([query_scale, 1.0, 1.0], dtype=jnp.float32).reshape(1, 3, 1, 1, 1)
    qkv_cols = qkv_full.reshape(width, 3, width)
    inputs = tokens.astype(jnp.float32)
    normed_one, hat_one, inv_one = layer_norm(inputs, gain_one, offset_one)
    first_low = normed_one.astype(jnp.bfloat16)
    per_device = num_heads // lax.axis_size("seq")
    head_start = lax.axis_index("seq") * per_device
    qkv_local = (
        jnp.einsum("brwc,ctd->btrwd", first_low, qkv_cols, preferred_element_type=jnp.float32)
        * factors
    ).astype(jnp.bfloat16)
    qkv_heads = lax.all_to_all(qkv_local, "seq", split_axis=4, concat_axis=2, tiled=True)
    qkv_heads = jnp.roll(qkv_heads, -SHIFT, axis=2)
    rel_bias = table_bias(
        lax.dynamic_slice_in_dim(table_full, head_start, per_device, 0), relative_index
    )
    mask_add = make_mask(region_ids)
    attn_heads, kept_state = attend_forward(qkv_heads, rel_bias, mask_add, per_device)
    attn_heads = jnp.roll(attn_heads, SHIFT, axis=1)
    attended = lax.all_to_all(attn_heads, "seq", split_axis=1, concat_axis=3, tiled=True)
    middle = inputs + jnp.einsum(
        "brwc,cd->brwd", attended, proj_full, preferred_element_type=jnp.float32
    )
    normed_two, hat_two, inv_two = layer_norm(middle, gain_two, offset_two)
    second_low = normed_two.astype(jnp.bfloat16)
    hidden = jnp.einsum(
        "brwc,cf->brwf", second_low, expand_full, preferred_element_type=jnp.float32
    )
    activated, slope = gelu_parts(hidden)
    act_low = activated.astype(jnp.bfloat16)
    output = (
        middle
        + jnp.einsum("brwf,fc->brwc", act_low, reduce_full, preferred_element_type=jnp.float32)
    ).astype(jnp.bfloat16)
    reduce_grad = jnp.einsum(
        "brwf,brwc->fc", act_low, cotangent, preferred_element_type=jnp.float32
    )
    hidden_grad = (
        jnp.einsum("brwc,fc->brwf", cotangent, reduce_full, preferred_element_type=jnp.float32)
        * slope
    ).astype(jnp.bfloat16)
    expand_grad = jnp.einsum(
        "brwc,brwf->cf", second_low, hidden_grad, preferred_element_type=jnp.float32
    )
    upstream_two = jnp.einsum(
        "brwf,cf->brwc", hidden_grad, expand_full, preferred_element_type=jnp.float32
    )
    back_two, gain_two_grad, offset_two_grad = norm_back(upstream_two, hat_two, inv_two, gain_two)
    middle_grad = cotangent.astype(jnp.float32) + back_two
    middle_low = middle_grad.astype(jnp.bfloat16)
    proj_grad = jnp.einsum(
        "brwc,brwd->cd", attended, middle_low, preferred_element_type=jnp.float32
    )
    attended_grad = jnp.einsum(
        "brwd,cd->brwc", middle_low, proj_full, preferred_element_type=jnp.float32
    ).astype(jnp.bfloat16)
    grad_heads = lax.all_to_all(attended_grad, "seq", split_axis=3, concat_axis=1, tiled=True)
    grad_heads = jnp.roll(grad_heads, -SHIFT, axis=1)
    qkv_grad_heads, bias_grad = attend_backward(
        grad_heads, kept_state, rel_bias, mask_add, per_device
    )
    qkv_grad_heads = jnp.roll(qkv_grad_heads, SHIFT, axis=2)
    qkv_grad = lax.all_to_all(qkv_grad_heads, "seq", split_axis=2, concat_axis=4, tiled=True)
    table_part = table_grad(bias_grad, relative_index, entries)
    table_grads = lax.dynamic_update_slice(
        jnp.zeros((num_heads, entries), jnp.float32), table_part, (head_start, 0)
    )
    qkv_grad_w = jnp.einsum(
        "brwc,btrwd->ctd", first_low, qkv_grad, preferred_element_type=jnp.float32
    ).reshape(width, 3 * width)
    upstream_one = jnp.einsum(
        "btrwd,ctd->brwc", qkv_grad, qkv_cols, preferred_element_type=jnp.float32
    )
    back_one, gain_one_grad, offset_one_grad = norm_back(upstream_one, hat_one, inv_one, gain_one)
    tokens_grad = middle_grad + back_one
    shares = (
        lax.psum_scatter(
            gain_one_grad.astype(jnp.bfloat16), "fsdp", scatter_dimension=0, tiled=True
        ).astype(jnp.float32),
        lax.psum_scatter(
            offset_one_grad.astype(jnp.bfloat16), "fsdp", scatter_dimension=0, tiled=True
        ).astype(jnp.float32),
        lax.psum_scatter(
            qkv_grad_w.astype(jnp.bfloat16), "fsdp", scatter_dimension=0, tiled=True
        ).astype(jnp.float32),
        lax.psum_scatter(
            proj_grad.astype(jnp.bfloat16), "fsdp", scatter_dimension=0, tiled=True
        ).astype(jnp.float32),
        lax.psum_scatter(
            table_grads.astype(jnp.bfloat16), "fsdp", scatter_dimension=0, tiled=True
        ).astype(jnp.float32),
        lax.psum_scatter(
            gain_two_grad.astype(jnp.bfloat16), "fsdp", scatter_dimension=0, tiled=True
        ).astype(jnp.float32),
        lax.psum_scatter(
            offset_two_grad.astype(jnp.bfloat16), "fsdp", scatter_dimension=0, tiled=True
        ).astype(jnp.float32),
        lax.psum_scatter(
            expand_grad.astype(jnp.bfloat16), "fsdp", scatter_dimension=0, tiled=True
        ).astype(jnp.float32),
        lax.psum_scatter(
            reduce_grad.astype(jnp.bfloat16), "fsdp", scatter_dimension=0, tiled=True
        ).astype(jnp.float32),
    )
    totals = (
        lax.psum(shares[0].astype(jnp.bfloat16), "seq").astype(jnp.float32),
        lax.psum(shares[1].astype(jnp.bfloat16), "seq").astype(jnp.float32),
        lax.psum(shares[2].astype(jnp.bfloat16), "seq").astype(jnp.float32),
        lax.psum(shares[3].astype(jnp.bfloat16), "seq").astype(jnp.float32),
        lax.psum(shares[4].astype(jnp.bfloat16), "seq").astype(jnp.float32),
        lax.psum(shares[5].astype(jnp.bfloat16), "seq").astype(jnp.float32),
        lax.psum(shares[6].astype(jnp.bfloat16), "seq").astype(jnp.float32),
        lax.psum(shares[7].astype(jnp.bfloat16), "seq").astype(jnp.float32),
        lax.psum(shares[8].astype(jnp.bfloat16), "seq").astype(jnp.float32),
    )
    qkv_total = totals[2]
    proj_total = totals[3]
    expand_total = totals[7]
    reduce_total = totals[8]
    return (
        output,
        tokens_grad,
        totals[0],
        totals[1],
        qkv_total,
        proj_total,
        totals[4],
        totals[5],
        totals[6],
        expand_total,
        reduce_total,
    )


def solution(mesh):
    placed = (
        P("fsdp", "seq", None, None),
        P("fsdp", "seq", None, None),
        P(),
        P(),
        P("fsdp"),
        P("fsdp"),
        P("fsdp", None),
        P("fsdp", None),
        P("fsdp", None),
        P("fsdp"),
        P("fsdp"),
        P("fsdp", None),
        P("fsdp", None),
    )
    return jax.shard_map(
        shards,
        mesh=mesh,
        in_specs=placed,
        out_specs=(
            P("fsdp", "seq", None, None),
            P("fsdp", "seq", None, None),
            P("fsdp"),
            P("fsdp"),
            P("fsdp", None),
            P("fsdp", None),
            P("fsdp", None),
            P("fsdp"),
            P("fsdp"),
            P("fsdp", None),
            P("fsdp", None),
        ),
        check_vma=False,
    )
```

profile of v0, /device:TPU:0, one launch (start us, length us, event | category | flops | bytes accessed | tf_op | source)
XLA Modules:
  0.0 359.1 jit_solution(13753991665746310214)
XLA Ops:
  7.2 2.0 copy.98
  10.0 6.2 %all-gather = bf16[4,1,128]{2,1,0:T(2,128)(2,1)S(1)} all-gather(bf16[1,1,128]{2,1,0:T(2,128)(2,1)} %bitcast.275), channel_id=1, replica_groups=mesh['fsdp'=4,'seq'=8] {'fsdp'}, dimensions={0}, use_global_device_ids=true | all-gather | bytes 1280 | tf_op jit(solution)/shard_map/all_gather | solution.py:171
  16.2 5.4 %all-gather.1 = bf16[4,1,128]{2,1,0:T(2,128)(2,1)S(1)} all-gather(bf16[1,1,128]{2,1,0:T(2,128)(2,1)} %bitcast.276), channel_id=1, replica_groups=mesh['fsdp'=4,'seq'=8] {'fsdp'}, dimensions={0}, use_global_device_ids=true | all-gather | bytes 1280 | tf_op jit(solution)/shard_map/all_gather | solution.py:172
  22.0 10.7 %all-gather.9.cloned.1.call-done = bf16[512,1536]{0,1:T(8,128)(2,1)} async-done(((bf16[128,1536]{0,1:T(8,128)(2,1)}), bf16[512,1536]{0,1:T(8,128)(2,1)}) %all-gather.9.cloned.1.call-update) | async-done | bytes 1572880 | tf_op jit(solution)/shard_map/all_gather | solution.py:173
  32.7 2.9 fusion.22
  35.6 3.7 %copy.100 = bf16[1,3,7,28,512]{3,2,1,0,4:T(8,128)(2,1)S(1)} copy(bf16[1,3,7,28,512]{4,3,1,2,0:T(8,128)(2,1)} %fusion.22) | data formatting | bytes 1204224 | tf_op jit(solution)/shard_map/convert_element_type | solution.py:203
  39.4 4.6 %reshape.406 = bf16[8,2,18816]{2,1,0:T(2,128)(2,1)} reshape(bf16[512,1,3,7,28]{4,3,2,1,0:T(8,128)(2,1)S(1)} %bitcast.239) | data formatting | bytes 1204224
  44.0 5.6 %all-to-all-start = ((bf16[8,2,18816]{2,1,0:T(2,128)(2,1)}), bf16[8,2,18816]{2,1,0:T(2,128)(2,1)}, u32[]{:S(2)}, u32[]{:S(2)}) async-start(bf16[8,2,18816]{2,1,0:T(2,128)(2,1)} %reshape.406), calls=%async_computation | async-start | bytes 1204224 | tf_op jit(solution)/shard_map/all_to_all | solution.py:204
  50.4 5.4 %all-gather.2 = bf16[4,4,169]{2,1,0:T(4,128)(2,1)S(1)} all-gather(bf16[1,4,169]{2,1,0:T(4,128)(2,1)S(1)} %bitcast.272), channel_id=1, replica_groups=mesh['fsdp'=4,'seq'=8] {'fsdp'}, dimensions={0}, use_global_device_ids=true | all-gather | bytes 6760 | tf_op jit(solution)/shard_map/all_gather | solution.py:175
  58.4 7.9 %all-to-all-done = bf16[8,2,18816]{2,1,0:T(2,128)(2,1)} async-done(((bf16[8,2,18816]{2,1,0:T(2,128)(2,1)}), bf16[8,2,18816]{2,1,0:T(2,128)(2,1)}, u32[]{:S(2)}, u32[]{:S(2)}) %all-to-all-start) | async-done | bytes 602144 | tf_op jit(solution)/shard_map/all_to_all | solution.py:204
  66.3 5.0 %reshape.407 = bf16[512,1,3,7,28]{4,3,2,1,0:T(8,128)(2,1)S(1)} reshape(bf16[8,2,18816]{2,1,0:T(2,128)(2,1)} %all-to-all-done) | data formatting | bytes 1204224
  71.3 4.5 %copy.101 = bf16[1,3,7,28,8,64]{5,2,4,3,1,0:T(8,128)(2,1)} copy(bf16[1,3,7,28,8,64]{3,2,1,5,4,0:T(8,128)(2,1)S(1)} %bitcast.238) | data formatting | bytes 1204224 | tf_op jit(solution)/shard_map/all_to_all | solution.py:204
  75.8 2.4 all_to_all.51
  80.4 4.3 %reshape.357 = bf16[1,3,8,7,4,7,2,32]{7,6,3,2,5,4,1,0:T(2,128)(2,1)S(1)} reshape(bf16[1,3,56,28,64]{4,2,3,1,0:T(8,128)(2,1)} %fusion.27) | data formatting | bytes 1204224 | tf_op jit(solution)/shard_map/reshape | solution.py:42
  88.1 2.2 exponential_reduce_fusion
  92.1 1.6 copy.111
  93.7 1.5 copy.112
  95.2 2.2 reshape.364
  98.7 3.7 %all-to-all-start.1 = ((bf16[8,2,6272]{2,1,0:T(2,128)(2,1)}), bf16[8,2,6272]{2,1,0:T(2,128)(2,1)S(1)}, u32[]{:S(2)}, u32[]{:S(2)}) async-start(bf16[8,2,6272]{2,1,0:T(2,128)(2,1)} %reshape.408), calls=%async_computation.1 | async-start | bytes 401408 | tf_op jit(solution)/shard_map/all_to_all | solution.py:212
  102.4 5.1 %all-gather.3 = bf16[4,1,128]{2,1,0:T(2,128)(2,1)S(1)} all-gather(bf16[1,1,128]{2,1,0:T(2,128)(2,1)S(1)} %bitcast.277), channel_id=1, replica_groups=mesh['fsdp'=4,'seq'=8] {'fsdp'}, dimensions={0}, use_global_device_ids=true | all-gather | bytes 1280 | tf_op jit(solution)/shard_map/all_gather | solution.py:176
  107.4 5.0 %all-gather.4 = bf16[4,1,128]{2,1,0:T(2,128)(2,1)S(1)} all-gather(bf16[1,1,128]{2,1,0:T(2,128)(2,1)S(1)} %bitcast.278), channel_id=1, replica_groups=mesh['fsdp'=4,'seq'=8] {'fsdp'}, dimensions={0}, use_global_device_ids=true | all-gather | bytes 1280 | tf_op jit(solution)/shard_map/all_gather | solution.py:177
  112.5 7.9 %all_gather.31 = bf16[512,512]{1,0:T(8,128)(2,1)S(1)} all-gather(bf16[128,512]{1,0:T(8,128)(2,1)S(1)} %copy-done.22), channel_id=1, replica_groups=mesh['fsdp'=4,'seq'=8] {'fsdp'}, dimensions={0}, use_global_device_ids=true | all-gather | bytes 655360 | tf_op jit(solution)/shard_map/all_gather | solution.py:174
  121.9 4.0 %multiply_convert_fusion = (bf16[7,28,2048]{2,1,0:T(8,128)(2,1)}, f32[7,28,2048]{2,1,0:T(8,128)}) fusion(bf16[512,2048]{1,0:T(8,128)(2,1)} %all-gather.11.cloned.1.call-done, f32[1,7,28,512]{3,2,1,0:T(8,128)S(1)} %get-tuple-element.85, f32[512]{0:T(512)S(1)} %bitcast.270, f32[512]{0:T(512)S(1)} %bitcast.260, f32[7,28]{1,0:T(8,128)S(1)} %add_rsqrt_fusion, ...), kind=kOutput, calls=%fused_computation.25 | convolution fusion | flops 413550592 | bytes 4912672 | tf_op jit(solution)/shard_map/brwc,cf->brwf/dot_general | solution.py:218
  125.9 3.3 fusion.3
  132.7 3.4 bitcast_convert_fusion.1
  137.0 3.3 bitcast_convert_fusion
  141.4 1.7 copy.116
  143.1 1.9 reshape.410
  145.0 5.9 %all-to-all-start.2 = ((bf16[8,2,6272]{2,1,0:T(2,128)(2,1)}), bf16[8,2,6272]{2,1,0:T(2,128)(2,1)S(1)}, u32[]{:S(2)}, u32[]{:S(2)}) async-start(bf16[8,2,6272]{2,1,0:T(2,128)(2,1)} %reshape.410), calls=%async_computation.2 | async-start | bytes 401408 | tf_op jit(solution)/shard_map/all_to_all | solution.py:249
  152.6 6.9 %all-to-all-done.2 = bf16[8,2,6272]{2,1,0:T(2,128)(2,1)S(1)} async-done(((bf16[8,2,6272]{2,1,0:T(2,128)(2,1)}), bf16[8,2,6272]{2,1,0:T(2,128)(2,1)S(1)}, u32[]{:S(2)}, u32[]{:S(2)}) %all-to-all-start.2) | async-done | bytes 200736 | tf_op jit(solution)/shard_map/all_to_all | solution.py:249
  160.6 1.9 copy.117
  165.4 1.8 copy.119
  168.6 2.4 copy.126
  173.3 1.5 copy.121
  176.2 1.7 copy.123
  178.5 1.9 copy.127
  180.3 2.3 reshape.371
  185.5 19.8 %all_to_all.66 = bf16[8,2,18816]{2,1,0:T(2,128)(2,1)S(1)} all-to-all(bf16[8,2,18816]{2,1,0:T(2,128)(2,1)S(1)} %reshape.412), channel_id=1, replica_groups=mesh['fsdp'=4,'seq'=8] {'seq'}, dimensions={0} | all-to-all | bytes 1204224 | tf_op jit(solution)/shard_map/all_to_all | solution.py:255
  209.1 2.0 fusion
  213.1 9.0 %reduce-scatter.11.cloned.1.call-done = bf16[512,512]{1,0:T(8,128)(2,1)} async-done(((bf16[2048,512]{1,0:T(8,128)(2,1)}), bf16[512,512]{1,0:T(8,128)(2,1)}) %reduce-scatter.11.cloned.1.call-update) | async-done | bytes 524304 | tf_op jit(solution)/shard_map/reduce_scatter | solution.py:293
  222.1 30.6 %reduce-scatter.5.cloned.1.call-done = bf16[128,1536]{1,0:T(8,128)(2,1)} async-done(((bf16[512,1536]{1,0:T(8,128)(2,1)}), bf16[128,1536]{1,0:T(8,128)(2,1)}) %reduce-scatter.5.cloned.1.call-update) | async-done | bytes 393232 | tf_op jit(solution)/shard_map/reduce_scatter | solution.py:275
  252.7 2.9 fusion.32
  256.9 2.1 fusion.62
  259.1 10.5 %all-reduce.7 = (bf16[512]{0:T(512)(128)(2,1)S(1)}, bf16[512]{0:T(512)(128)(2,1)S(1)}, bf16[16,169]{1,0:T(8,128)(2,1)S(1)}, bf16[512]{0:T(512)(128)(2,1)S(1)}, bf16[512]{0:T(512)(128)(2,1)S(1)}) all-reduce(bf16[512]{0:T(512)(128)(2,1)S(1)} %get-tuple-element.57, ...), channel_id=2, replica_groups=mesh['fsdp'=4,'seq'=8] {'fsdp'}, use_global_device_ids=true, to_apply=%region_11.12.clone | all-reduce | flops 4752 | bytes 19008
  270.0 21.9 %all-reduce.5 = (bf16[128]{0:T(256)(128)(2,1)S(1)}, bf16[128]{0:T(256)(128)(2,1)S(1)}, bf16[4,169]{1,0:T(4,128)(2,1)S(1)}, bf16[128]{0:T(256)(128)(2,1)S(1)}, bf16[128]{0:T(256)(128)(2,1)S(1)}) all-reduce(bf16[128]{0:T(256)(128)(2,1)S(1)} %dynamic-slice.1, ...), channel_id=1, replica_groups=mesh['fsdp'=4,'seq'=8] {'seq'}, use_global_device_ids=true, to_apply=%region_12.13 | all-reduce | flops 1188 | bytes 4752 | tf_op jit(solution)/shard_map/psum | solution.py:298
  295.9 50.3 %all-reduce.10.cloned.1.call-done = (bf16[128,1536]{1,0:T(8,128)(2,1)}, bf16[128,512]{1,0:T(8,128)(2,1)}, bf16[128,2048]{1,0:T(8,128)(2,1)}, bf16[512,512]{1,0:T(8,128)(2,1)}) async-done(((bf16[128,1536]{1,0:T(8,128)(2,1)}, bf16[128,512]{1,0:T(8,128)(2,1)}, bf16[128,2048]{1,0:T(8,128)(2,1)}, bf16[512,512]{1,0:T(8,128)(2,1)}), (bf16[128,1536]{1,0:T(8,128)(2,1)}, bf16[128,512]{1,0:T(8,128)(2,1)}, ...) | async-done | bytes 1572880 | tf_op jit(solution)/shard_map/psum | solution.py:300
  346.2 1.7 convert_element_type.178
  347.9 2.0 convert_element_type.176
  (186 shorter events, 46.2 us)
Async XLA Ops:
  7.2 25.5 %copy-start.34 = (f32[3]{0:T(128)S(1)}, f32[3]{0:T(128)}, u32[]{:S(2)}) copy-start(f32[3]{0:T(128)} %constant.41.clone) | copy-start | bytes 40
  7.2 14.5 %copy-start.7 = (bf16[1,7,28,512]{3,2,1,0:T(8,128)(2,1)S(1)}, bf16[1,7,28,512]{3,2,1,0:T(8,128)(2,1)}, u32[]{:S(2)}) copy-start(bf16[1,7,28,512]{3,2,1,0:T(8,128)(2,1)} %param.14) | copy-start | bytes 602116
  7.2 25.5 %all-gather.9.cloned.1.call-start = ((), (), s32[]{:S(2)}) async-start(), calls=%async_computation.8 | async-start | bytes 1966080 | tf_op jit(solution)/shard_map/all_gather | solution.py:173
  9.2 112.7 %all-gather.11.cloned.1.call-start = ((), (), s32[]{:S(2)}) async-start(), calls=%async_computation.9 | async-start | bytes 2621440 | tf_op jit(solution)/shard_map/all_gather | solution.py:178
  21.6 11.1 %copy-start.26 = (f32[4,1,128]{2,1,0:T(1,128)}, f32[4,1,128]{2,1,0:T(1,128)S(1)}, u32[]{:S(2)}) copy-start(f32[4,1,128]{2,1,0:T(1,128)S(1)} %convert_element_type.190) | copy-start | bytes 6148
  39.4 11.0 %copy-start.25 = (bf16[4,169]{1,0:T(4,128)(2,1)S(1)}, bf16[4,169]{1,0:T(4,128)(2,1)}, u32[]{:S(2)}) copy-start(bf16[4,169]{1,0:T(4,128)(2,1)} %param.22) | copy-start | bytes 4060
  39.4 16.4 %copy-start.31 = (s32[49,49]{1,0:T(8,128)S(1)}, s32[49,49]{1,0:T(8,128)}, u32[]{:S(2)}) copy-start(s32[49,49]{1,0:T(8,128)} %param.17) | copy-start | bytes 28816
  44.0 12.7 %copy-start.23 = (s32[56,28]{0,1:T(8,128)S(1)}, s32[56,28]{0,1:T(8,128)}, u32[]{:S(2)}) copy-start(s32[56,28]{0,1:T(8,128)} %param.16) | copy-start | bytes 18820
  44.0 22.3 %all-to-all-start = ((bf16[8,2,18816]{2,1,0:T(2,128)(2,1)}), bf16[8,2,18816]{2,1,0:T(2,128)(2,1)}, u32[]{:S(2)}, u32[]{:S(2)}) async-start(bf16[8,2,18816]{2,1,0:T(2,128)(2,1)} %reshape.406), calls=%async_computation | async-start | bytes 1204224 | tf_op jit(solution)/shard_map/all_to_all | solution.py:204
  49.6 76.3 %all-gather.13.cloned.1.call-start = ((), (), s32[]{:S(2)}) async-start(), calls=%async_computation.10 | async-start | bytes 2621440 | tf_op jit(solution)/shard_map/all_gather | solution.py:179
  87.3 2.9 copy-start.2
  88.1 2.2 copy-start
  88.1 2.8 copy-start.13
  97.4 5.0 %copy-start.29 = (bf16[128]{0:T(256)(128)(2,1)S(1)}, bf16[128]{0:T(256)(128)(2,1)}, u32[]{:S(2)}) copy-start(bf16[128]{0:T(256)(128)(2,1)} %param.23) | copy-start | bytes 772
  97.4 10.1 %copy-start.30 = (bf16[128]{0:T(256)(128)(2,1)S(1)}, bf16[128]{0:T(256)(128)(2,1)}, u32[]{:S(2)}) copy-start(bf16[128]{0:T(256)(128)(2,1)} %param.24) | copy-start | bytes 772
  97.4 15.1 %copy-start.22 = (bf16[128,512]{1,0:T(8,128)(2,1)S(1)}, bf16[128,512]{1,0:T(8,128)(2,1)}, u32[]{:S(2)}) copy-start(bf16[128,512]{1,0:T(8,128)(2,1)} %param.21) | copy-start | bytes 393220
  98.7 21.8 %all-to-all-start.1 = ((bf16[8,2,6272]{2,1,0:T(2,128)(2,1)}), bf16[8,2,6272]{2,1,0:T(2,128)(2,1)S(1)}, u32[]{:S(2)}, u32[]{:S(2)}) async-start(bf16[8,2,6272]{2,1,0:T(2,128)(2,1)} %reshape.408), calls=%async_computation.1 | async-start | bytes 401408 | tf_op jit(solution)/shard_map/all_to_all | solution.py:212
  102.3 110.7 %reduce-scatter.7.cloned.1.call-start = ((), (), s32[]{:S(2)}) async-start(), calls=%async_computation.12 | async-start | bytes 655360 | tf_op jit(solution)/shard_map/reduce_scatter | solution.py:278
  112.5 8.8 %copy-start.8 = (bf16[1,7,28,512]{3,2,1,0:T(8,128)(2,1)S(1)}, bf16[1,7,28,512]{3,2,1,0:T(8,128)(2,1)}, u32[]{:S(2)}) copy-start(bf16[1,7,28,512]{3,2,1,0:T(8,128)(2,1)} %param.14) | copy-start | bytes 602116
  121.9 4.0 %copy-start.18 = (bf16[1,7,28,512]{3,2,1,0:T(8,128)(2,1)S(1)}, bf16[1,7,28,512]{3,2,1,0:T(8,128)(2,1)}, u32[]{:S(2)}) copy-start(bf16[1,7,28,512]{3,2,1,0:T(8,128)(2,1)} %param.15) | copy-start | bytes 602116
  125.9 3.3 copy-start.12
  129.2 1.4 copy-start.35
  129.3 2.0 copy-start.19
  131.5 8.8 %copy-start.4 = (f32[1,7,28,512]{3,2,1,0:T(8,128)}, f32[1,7,28,512]{3,2,1,0:T(8,128)S(1)}, u32[]{:S(2)}) copy-start(f32[1,7,28,512]{3,2,1,0:T(8,128)S(1)} %fusion.67) | copy-start | bytes 1204228
  132.7 80.4 %reduce-scatter.9.cloned.1.call-start = ((), (), s32[]{:S(2)}) async-start(), calls=%async_computation.13 | async-start | bytes 2621440 | tf_op jit(solution)/shard_map/reduce_scatter | solution.py:290
  136.1 0.9 copy-start.20
  136.1 86.0 %reduce-scatter.11.cloned.1.call-start = ((), (), s32[]{:S(2)}) async-start(), calls=%async_computation.14 | async-start | bytes 2621440 | tf_op jit(solution)/shard_map/reduce_scatter | solution.py:293
  145.0 14.5 %all-to-all-start.2 = ((bf16[8,2,6272]{2,1,0:T(2,128)(2,1)}), bf16[8,2,6272]{2,1,0:T(2,128)(2,1)S(1)}, u32[]{:S(2)}, u32[]{:S(2)}) async-start(bf16[8,2,6272]{2,1,0:T(2,128)(2,1)} %reshape.410), calls=%async_computation.2 | async-start | bytes 401408 | tf_op jit(solution)/shard_map/all_to_all | solution.py:249
  150.9 101.7 %reduce-scatter.5.cloned.1.call-start = ((), (), s32[]{:S(2)}) async-start(), calls=%async_computation.11 | async-start | bytes 1966080 | tf_op jit(solution)/shard_map/reduce_scatter | solution.py:275
  164.1 3.1 copy-start.15
  167.2 3.8 %copy-start.14 = (bf16[1,1,8,4,2,49,32]{5,6,4,3,2,1,0:T(8,128)(2,1)S(1)}, bf16[1,1,8,4,2,49,32]{5,6,4,3,2,1,0:T(8,128)(2,1)}, u32[]{:S(2)}) copy-start(bf16[1,1,8,4,2,49,32]{5,6,4,3,2,1,0:T(8,128)(2,1)} %copy.151) | copy-start | bytes 602116
  171.9 1.0 copy-start.3
  172.5 2.3 copy-start.1
  174.8 3.1 copy-start.10
  176.2 1.7 copy-start.11
  182.7 0.9 slice-start
  182.7 1.3 slice-start.1
  207.7 1.4 copy-start.9
  207.7 1.4 copy-start.27
  209.1 2.1 copy-start.33
  211.1 41.6 %copy-start.6 = (bf16[7,28,2048]{2,1,0:T(8,128)(2,1)S(1)}, bf16[7,28,2048]{2,1,0:T(8,128)(2,1)}, u32[]{:S(2)}) copy-start(bf16[7,28,2048]{2,1,0:T(8,128)(2,1)} %get-tuple-element.86) | copy-start | bytes 2408452
  211.1 135.1 %all-reduce.10.cloned.1.call-start = ((), (), s32[]{:S(2)}) async-start(), calls=%async_computation.15 | async-start | bytes 3145728 | tf_op jit(solution)/shard_map/psum | solution.py:300
  252.7 3.1 copy-start.32
  256.8 2.3 copy-start.24
  256.8 2.3 copy-start.28
  256.9 37.6 %copy-start.5 = (f32[1,7,28,512]{3,2,1,0:T(8,128)S(1)}, f32[1,7,28,512]{3,2,1,0:T(8,128)}, u32[]{:S(2)}) copy-start(f32[1,7,28,512]{3,2,1,0:T(8,128)} %copy-done.4) | copy-start | bytes 1204228
  346.2 3.7 %copy-start.17 = (bf16[128,2048]{1,0:T(8,128)(2,1)S(1)}, bf16[128,2048]{1,0:T(8,128)(2,1)}, u32[]{:S(2)}) copy-start(bf16[128,2048]{1,0:T(8,128)(2,1)} %get-tuple-element.70) | copy-start | bytes 1572868
  346.2 4.7 %copy-start.16 = (bf16[512,512]{1,0:T(8,128)(2,1)S(1)}, bf16[512,512]{1,0:T(8,128)(2,1)}, u32[]{:S(2)}) copy-start(bf16[512,512]{1,0:T(8,128)(2,1)} %get-tuple-element.71) | copy-start | bytes 1572868
  (1 other events, 0.6 us)
Sparse Core Ops, SparseCore 0:
  10.1 22.5 all-gather.8
  34.3 22.5 all-gather.10
  58.5 22.5 all-gather.12
  132.8 22.0 reduce-scatter.6
  157.2 31.1 reduce-scatter.8
  190.8 31.1 reduce-scatter.10
  224.6 28.0 reduce-scatter.4
  256.5 89.6 all-reduce.9
where the time goes:
time: 364 us; the launch traced here: 359 us
  waiting for transfers between devices  117 us (32%)
  blocking collectives  87.2 us (24%)
  local copies, waits for them, and re-layouts  70.8 us (19%)
  matrix products  37 us (10%)
  between operations  16.5 us (5%)
  starting transfers between devices  15.7 us (4%)
  other arithmetic  15.1 us (4%)
    psum x1, waiting for transfers between devices, shards(): lax.psum(shares[2].astype(jnp.bfloat16), 'seq').astype(jnp.float32)  50.3 us
    reduce_scatter x1, waiting for transfers between devices, shards(): lax.psum_scatter(qkv_grad_w.astype(jnp.bfloat16), 'fsdp', scatter_dimensi...  30.6 us
    unnamed x92, local copies, waits for them, and re-layouts  24.5 us
    psum x1, blocking collectives, shards(): lax.psum(shares[0].astype(jnp.bfloat16), 'seq').astype(jnp.float32)  21.9 us
    all_to_all x1, blocking collectives, shards(): lax.all_to_all(qkv_grad_heads, 'seq', split_axis=2, concat_axis=4, tiled=...  19.8 us
    all_gather x1, waiting for transfers between devices, shards(): lax.all_gather(qkv_weight, 'fsdp', axis=0, tiled=True)  10.7 us
    unnamed x1, blocking collectives  10.5 us
    reduce_scatter x1, waiting for transfers between devices, shards(): lax.psum_scatter(reduce_grad.astype(jnp.bfloat16), 'fsdp', scatter_dimens...  8.96 us
  transfers between devices with their start and end apart: 11, of which 6 were waited for; matrix products, arithmetic and copies ran while one was open for 28% of the time, Pallas kernels for 0%

commit v1 on v0

--- a/solution.py
+++ b/solution.py
@@ -252,7 +252,12 @@
         grad_heads, kept_state, rel_bias, mask_add, per_device
     )
     qkv_grad_heads = jnp.roll(qkv_grad_heads, SHIFT, axis=2)
-    qkv_grad = lax.all_to_all(qkv_grad_heads, "seq", split_axis=2, concat_axis=4, tiled=True)
+    qkv_grad = jnp.concatenate(
+        lax.all_to_all(
+            jnp.stack(jnp.split(qkv_grad_heads, lax.axis_size("seq"), axis=2)), "seq", 0, 0
+        ),
+        axis=4,
+    )
     table_part = table_grad(bias_grad, relative_index, entries)
     table_grads = lax.dynamic_update_slice(
         jnp.zeros((num_heads, entries), jnp.float32), table_part, (head_start, 0)

time: 364 us -> 364 us (level)
    unnamed x92 -> x98, local copies, waits for them, and re-layouts: 24.5 us -> 23.2 us
  transfers between devices with their start and end apart: 11 -> 11, of which waited for: 6 -> 6; matrix products, arithmetic and copies ran while one was open for 28% -> 29% of each run, Pallas kernels for 0% -> 0%
where the time goes in v1:
time: 364 us; the launch traced here: 359 us
  waiting for transfers between devices  117 us (32%)
  blocking collectives  86.9 us (24%)
  local copies, waits for them, and re-layouts  69.6 us (19%)
  matrix products  37 us (10%)
  between operations  16.5 us (5%)
  other arithmetic  16.2 us (4%)
  starting transfers between devices  15.7 us (4%)
    psum x1, waiting for transfers between devices, shards(): lax.psum(shares[2].astype(jnp.bfloat16), 'seq').astype(jnp.float32)  50.3 us
    reduce_scatter x1, waiting for transfers between devices, shards(): lax.psum_scatter(qkv_grad_w.astype(jnp.bfloat16), 'fsdp', scatter_dimensi...  30.6 us
    unnamed x98, local copies, waits for them, and re-layouts  23.2 us
    psum x1, blocking collectives, shards(): lax.psum(shares[0].astype(jnp.bfloat16), 'seq').astype(jnp.float32)  21.9 us
    all_to_all x1, blocking collectives, shards(): lax.all_to_all(jnp.stack(jnp.split(qkv_grad_heads, lax.axis_size('seq'),...  19.5 us
    reduce_scatter x1, waiting for transfers between devices, shards(): lax.psum_scatter(reduce_grad.astype(jnp.bfloat16), 'fsdp', scatter_dimens...  11.2 us
    all_gather x1, waiting for transfers between devices, shards(): lax.all_gather(qkv_weight, 'fsdp', axis=0, tiled=True)  10.7 us
    unnamed x1, blocking collectives  10.5 us
  transfers between devices with their start and end apart: 11, of which 6 were waited for; matrix products, arithmetic and copies ran while one was open for 29% of the time, Pallas kernels for 0%

profile of v1, /device:TPU:0, one launch (start us, length us, event | category | flops | bytes accessed | tf_op | source)
XLA Modules:
  0.0 359.1 jit_solution(6817626767328594070)
XLA Ops:
  7.2 2.0 copy.107
  10.0 6.2 %all-gather = bf16[4,1,128]{2,1,0:T(2,128)(2,1)S(1)} all-gather(bf16[1,1,128]{2,1,0:T(2,128)(2,1)} %bitcast.290), channel_id=1, replica_groups=mesh['fsdp'=4,'seq'=8] {'fsdp'}, dimensions={0}, use_global_device_ids=true | all-gather | bytes 1280 | tf_op jit(solution)/shard_map/all_gather | solution.py:171
  16.2 5.4 %all-gather.1 = bf16[4,1,128]{2,1,0:T(2,128)(2,1)S(1)} all-gather(bf16[1,1,128]{2,1,0:T(2,128)(2,1)} %bitcast.291), channel_id=1, replica_groups=mesh['fsdp'=4,'seq'=8] {'fsdp'}, dimensions={0}, use_global_device_ids=true | all-gather | bytes 1280 | tf_op jit(solution)/shard_map/all_gather | solution.py:172
  22.0 10.7 %all-gather.9.cloned.1.call-done = bf16[512,1536]{0,1:T(8,128)(2,1)} async-done(((bf16[128,1536]{0,1:T(8,128)(2,1)}), bf16[512,1536]{0,1:T(8,128)(2,1)}) %all-gather.9.cloned.1.call-update) | async-done | bytes 1572880 | tf_op jit(solution)/shard_map/all_gather | solution.py:173
  32.7 2.9 fusion.22
  35.6 3.7 %copy.109 = bf16[1,3,7,28,512]{3,2,1,0,4:T(8,128)(2,1)S(1)} copy(bf16[1,3,7,28,512]{4,3,1,2,0:T(8,128)(2,1)} %fusion.22) | data formatting | bytes 1204224 | tf_op jit(solution)/shard_map/convert_element_type | solution.py:203
  39.4 4.6 %reshape.411 = bf16[8,2,18816]{2,1,0:T(2,128)(2,1)} reshape(bf16[512,1,3,7,28]{4,3,2,1,0:T(8,128)(2,1)S(1)} %bitcast.256) | data formatting | bytes 1204224
  44.0 5.6 %all-to-all-start = ((bf16[8,2,18816]{2,1,0:T(2,128)(2,1)}), bf16[8,2,18816]{2,1,0:T(2,128)(2,1)}, u32[]{:S(2)}, u32[]{:S(2)}) async-start(bf16[8,2,18816]{2,1,0:T(2,128)(2,1)} %reshape.411), calls=%async_computation | async-start | bytes 1204224 | tf_op jit(solution)/shard_map/all_to_all | solution.py:204
  50.4 5.4 %all-gather.2 = bf16[4,4,169]{2,1,0:T(4,128)(2,1)S(1)} all-gather(bf16[1,4,169]{2,1,0:T(4,128)(2,1)S(1)} %bitcast.287), channel_id=1, replica_groups=mesh['fsdp'=4,'seq'=8] {'fsdp'}, dimensions={0}, use_global_device_ids=true | all-gather | bytes 6760 | tf_op jit(solution)/shard_map/all_gather | solution.py:175
  58.4 7.9 %all-to-all-done = bf16[8,2,18816]{2,1,0:T(2,128)(2,1)} async-done(((bf16[8,2,18816]{2,1,0:T(2,128)(2,1)}), bf16[8,2,18816]{2,1,0:T(2,128)(2,1)}, u32[]{:S(2)}, u32[]{:S(2)}) %all-to-all-start) | async-done | bytes 602144 | tf_op jit(solution)/shard_map/all_to_all | solution.py:204
  66.3 5.0 %reshape.412 = bf16[512,1,3,7,28]{4,3,2,1,0:T(8,128)(2,1)S(1)} reshape(bf16[8,2,18816]{2,1,0:T(2,128)(2,1)} %all-to-all-done) | data formatting | bytes 1204224
  71.3 4.5 %copy.110 = bf16[1,3,7,28,8,64]{5,2,4,3,1,0:T(8,128)(2,1)} copy(bf16[1,3,7,28,8,64]{3,2,1,5,4,0:T(8,128)(2,1)S(1)} %bitcast.255) | data formatting | bytes 1204224 | tf_op jit(solution)/shard_map/all_to_all | solution.py:204
  75.8 2.4 all_to_all.43
  80.3 4.3 %reshape.361 = bf16[1,3,8,7,4,7,2,32]{7,6,3,2,5,4,1,0:T(2,128)(2,1)S(1)} reshape(bf16[1,3,56,28,64]{4,2,3,1,0:T(8,128)(2,1)} %fusion.27) | data formatting | bytes 1204224 | tf_op jit(solution)/shard_map/reshape | solution.py:42
  85.1 1.5 copy.160
  88.0 2.2 exponential_reduce_fusion
  91.4 1.6 copy.120
  93.0 1.5 copy.121
  94.5 2.2 reshape.368
  98.0 3.6 %all-to-all-start.1 = ((bf16[8,2,6272]{2,1,0:T(2,128)(2,1)}), bf16[8,2,6272]{2,1,0:T(2,128)(2,1)S(1)}, u32[]{:S(2)}, u32[]{:S(2)}) async-start(bf16[8,2,6272]{2,1,0:T(2,128)(2,1)} %reshape.413), calls=%async_computation.1 | async-start | bytes 401408 | tf_op jit(solution)/shard_map/all_to_all | solution.py:212
  101.7 5.1 %all-gather.3 = bf16[4,1,128]{2,1,0:T(2,128)(2,1)S(1)} all-gather(bf16[1,1,128]{2,1,0:T(2,128)(2,1)S(1)} %bitcast.292), channel_id=1, replica_groups=mesh['fsdp'=4,'seq'=8] {'fsdp'}, dimensions={0}, use_global_device_ids=true | all-gather | bytes 1280 | tf_op jit(solution)/shard_map/all_gather | solution.py:176
  106.8 5.0 %all-gather.4 = bf16[4,1,128]{2,1,0:T(2,128)(2,1)S(1)} all-gather(bf16[1,1,128]{2,1,0:T(2,128)(2,1)S(1)} %bitcast.293), channel_id=1, replica_groups=mesh['fsdp'=4,'seq'=8] {'fsdp'}, dimensions={0}, use_global_device_ids=true | all-gather | bytes 1280 | tf_op jit(solution)/shard_map/all_gather | solution.py:177
  112.4 7.9 %all_gather.31 = bf16[512,512]{1,0:T(8,128)(2,1)S(1)} all-gather(bf16[128,512]{1,0:T(8,128)(2,1)S(1)} %copy-done.20), channel_id=1, replica_groups=mesh['fsdp'=4,'seq'=8] {'fsdp'}, dimensions={0}, use_global_device_ids=true | all-gather | bytes 655360 | tf_op jit(solution)/shard_map/all_gather | solution.py:174
  121.8 4.0 %multiply_convert_fusion = (bf16[7,28,2048]{2,1,0:T(8,128)(2,1)}, f32[7,28,2048]{2,1,0:T(8,128)}) fusion(bf16[512,2048]{1,0:T(8,128)(2,1)} %all-gather.11.cloned.1.call-done, f32[1,7,28,512]{3,2,1,0:T(8,128)S(1)} %get-tuple-element.85, f32[512]{0:T(512)S(1)} %bitcast.286, f32[512]{0:T(512)S(1)} %bitcast.275, f32[7,28]{1,0:T(8,128)S(1)} %add_rsqrt_fusion, ...), kind=kOutput, calls=%fused_computation.32 | convolution fusion | flops 413550592 | bytes 4912672 | tf_op jit(solution)/shard_map/brwc,cf->brwf/dot_general | solution.py:218
  125.8 3.3 fusion.3
  132.7 3.4 bitcast_convert_fusion.1
  137.8 1.8 copy.125
  139.5 1.9 reshape.415
  141.5 5.9 %all-to-all-start.2 = ((bf16[8,2,6272]{2,1,0:T(2,128)(2,1)}), bf16[8,2,6272]{2,1,0:T(2,128)(2,1)S(1)}, u32[]{:S(2)}, u32[]{:S(2)}) async-start(bf16[8,2,6272]{2,1,0:T(2,128)(2,1)} %reshape.415), calls=%async_computation.2 | async-start | bytes 401408 | tf_op jit(solution)/shard_map/all_to_all | solution.py:249
  147.4 3.4 bitcast_convert_fusion
  151.0 4.9 %all-to-all-done.2 = bf16[8,2,6272]{2,1,0:T(2,128)(2,1)S(1)} async-done(((bf16[8,2,6272]{2,1,0:T(2,128)(2,1)}), bf16[8,2,6272]{2,1,0:T(2,128)(2,1)S(1)}, u32[]{:S(2)}, u32[]{:S(2)}) %all-to-all-start.2) | async-done | bytes 200736 | tf_op jit(solution)/shard_map/all_to_all | solution.py:249
  157.0 1.9 copy.126
  161.9 2.0 copy.128
  165.2 2.5 copy.135
  172.8 1.7 copy.132
  175.0 1.9 copy.136
  176.9 2.5 reshape.375
  183.7 19.5 %all_to_all.56 = bf16[8,2,18816]{2,1,0:T(2,128)(2,1)S(1)} all-to-all(bf16[8,2,18816]{2,1,0:T(2,128)(2,1)S(1)} %reshape.417), channel_id=1, replica_groups=mesh['fsdp'=4,'seq'=8] {'seq'}, dimensions={0} | all-to-all | bytes 1204224 | tf_op jit(solution)/shard_map/all_to_all | solution.py:256
  206.9 1.9 fusion
  210.8 11.2 %reduce-scatter.11.cloned.1.call-done = bf16[512,512]{1,0:T(8,128)(2,1)} async-done(((bf16[2048,512]{1,0:T(8,128)(2,1)}), bf16[512,512]{1,0:T(8,128)(2,1)}) %reduce-scatter.11.cloned.1.call-update) | async-done | bytes 524304 | tf_op jit(solution)/shard_map/reduce_scatter | solution.py:298
  222.0 30.6 %reduce-scatter.5.cloned.1.call-done = bf16[128,1536]{1,0:T(8,128)(2,1)} async-done(((bf16[512,1536]{1,0:T(8,128)(2,1)}), bf16[128,1536]{1,0:T(8,128)(2,1)}) %reduce-scatter.5.cloned.1.call-update) | async-done | bytes 393232 | tf_op jit(solution)/shard_map/reduce_scatter | solution.py:280
  252.7 2.9 fusion.32
  256.8 2.1 fusion.62
  259.1 10.5 %all-reduce.7 = (bf16[512]{0:T(512)(128)(2,1)S(1)}, bf16[512]{0:T(512)(128)(2,1)S(1)}, bf16[16,169]{1,0:T(8,128)(2,1)S(1)}, bf16[512]{0:T(512)(128)(2,1)S(1)}, bf16[512]{0:T(512)(128)(2,1)S(1)}) all-reduce(bf16[512]{0:T(512)(128)(2,1)S(1)} %get-tuple-element.57, ...), channel_id=2, replica_groups=mesh['fsdp'=4,'seq'=8] {'fsdp'}, use_global_device_ids=true, to_apply=%region_11.12.clone | all-reduce | flops 4752 | bytes 19008
  269.9 21.9 %all-reduce.5 = (bf16[128]{0:T(256)(128)(2,1)S(1)}, bf16[128]{0:T(256)(128)(2,1)S(1)}, bf16[4,169]{1,0:T(4,128)(2,1)S(1)}, bf16[128]{0:T(256)(128)(2,1)S(1)}, bf16[128]{0:T(256)(128)(2,1)S(1)}) all-reduce(bf16[128]{0:T(256)(128)(2,1)S(1)} %dynamic-slice.1, ...), channel_id=1, replica_groups=mesh['fsdp'=4,'seq'=8] {'seq'}, use_global_device_ids=true, to_apply=%region_12.13 | all-reduce | flops 1188 | bytes 4752 | tf_op jit(solution)/shard_map/psum | solution.py:303
  295.8 50.3 %all-reduce.10.cloned.1.call-done = (bf16[128,1536]{1,0:T(8,128)(2,1)}, bf16[128,512]{1,0:T(8,128)(2,1)}, bf16[128,2048]{1,0:T(8,128)(2,1)}, bf16[512,512]{1,0:T(8,128)(2,1)}) async-done(((bf16[128,1536]{1,0:T(8,128)(2,1)}, bf16[128,512]{1,0:T(8,128)(2,1)}, bf16[128,2048]{1,0:T(8,128)(2,1)}, bf16[512,512]{1,0:T(8,128)(2,1)}), (bf16[128,1536]{1,0:T(8,128)(2,1)}, bf16[128,512]{1,0:T(8,128)(2,1)}, ...) | async-done | bytes 1572880 | tf_op jit(solution)/shard_map/psum | solution.py:305
  346.1 1.7 convert_element_type.178
  347.9 2.0 convert_element_type.176
  (197 shorter events, 45.9 us)
Async XLA Ops:
  7.2 25.5 %copy-start.37 = (f32[3]{0:T(128)S(1)}, f32[3]{0:T(128)}, u32[]{:S(2)}) copy-start(f32[3]{0:T(128)} %constant.41.clone) | copy-start | bytes 40
  7.2 14.5 %copy-start.7 = (bf16[1,7,28,512]{3,2,1,0:T(8,128)(2,1)S(1)}, bf16[1,7,28,512]{3,2,1,0:T(8,128)(2,1)}, u32[]{:S(2)}) copy-start(bf16[1,7,28,512]{3,2,1,0:T(8,128)(2,1)} %param.14) | copy-start | bytes 602116
  7.2 25.5 %all-gather.9.cloned.1.call-start = ((), (), s32[]{:S(2)}) async-start(), calls=%async_computation.8 | async-start | bytes 1966080 | tf_op jit(solution)/shard_map/all_gather | solution.py:173
  9.2 112.5 %all-gather.11.cloned.1.call-start = ((), (), s32[]{:S(2)}) async-start(), calls=%async_computation.9 | async-start | bytes 2621440 | tf_op jit(solution)/shard_map/all_gather | solution.py:178
  16.2 16.5 %copy-start.21 = (f32[4,1,128]{2,1,0:T(1,128)}, f32[4,1,128]{2,1,0:T(1,128)S(1)}, u32[]{:S(2)}) copy-start(f32[4,1,128]{2,1,0:T(1,128)S(1)} %convert_element_type.189) | copy-start | bytes 6148
  21.7 11.1 %copy-start.29 = (f32[4,1,128]{2,1,0:T(1,128)}, f32[4,1,128]{2,1,0:T(1,128)S(1)}, u32[]{:S(2)}) copy-start(f32[4,1,128]{2,1,0:T(1,128)S(1)} %convert_element_type.190) | copy-start | bytes 6148
  22.0 10.7 %copy-start.23 = (f32[7,28]{1,0:T(8,128)}, f32[7,28]{1,0:T(8,128)S(1)}, u32[]{:S(2)}) copy-start(f32[7,28]{1,0:T(8,128)S(1)} %add_rsqrt_fusion.1) | copy-start | bytes 2356
  39.4 11.0 %copy-start.28 = (bf16[4,169]{1,0:T(4,128)(2,1)S(1)}, bf16[4,169]{1,0:T(4,128)(2,1)}, u32[]{:S(2)}) copy-start(bf16[4,169]{1,0:T(4,128)(2,1)} %param.22) | copy-start | bytes 4060
  39.4 16.4 %copy-start.34 = (s32[49,49]{1,0:T(8,128)S(1)}, s32[49,49]{1,0:T(8,128)}, u32[]{:S(2)}) copy-start(s32[49,49]{1,0:T(8,128)} %param.17) | copy-start | bytes 28816
  44.0 12.7 %copy-start.25 = (s32[56,28]{0,1:T(8,128)S(1)}, s32[56,28]{0,1:T(8,128)}, u32[]{:S(2)}) copy-start(s32[56,28]{0,1:T(8,128)} %param.16) | copy-start | bytes 18820
  44.0 22.3 %all-to-all-start = ((bf16[8,2,18816]{2,1,0:T(2,128)(2,1)}), bf16[8,2,18816]{2,1,0:T(2,128)(2,1)}, u32[]{:S(2)}, u32[]{:S(2)}) async-start(bf16[8,2,18816]{2,1,0:T(2,128)(2,1)} %reshape.411), calls=%async_computation | async-start | bytes 1204224 | tf_op jit(solution)/shard_map/all_to_all | solution.py:204
  49.6 76.2 %all-gather.13.cloned.1.call-start = ((), (), s32[]{:S(2)}) async-start(), calls=%async_computation.10 | async-start | bytes 2621440 | tf_op jit(solution)/shard_map/all_gather | solution.py:179
  87.3 2.9 copy-start.2
  88.0 2.2 copy-start
  88.0 2.2 copy-start.13
  96.7 5.0 %copy-start.32 = (bf16[128]{0:T(256)(128)(2,1)S(1)}, bf16[128]{0:T(256)(128)(2,1)}, u32[]{:S(2)}) copy-start(bf16[128]{0:T(256)(128)(2,1)} %param.23) | copy-start | bytes 772
  96.7 10.1 %copy-start.33 = (bf16[128]{0:T(256)(128)(2,1)S(1)}, bf16[128]{0:T(256)(128)(2,1)}, u32[]{:S(2)}) copy-start(bf16[128]{0:T(256)(128)(2,1)} %param.24) | copy-start | bytes 772
  96.7 15.7 %copy-start.20 = (bf16[128,512]{1,0:T(8,128)(2,1)S(1)}, bf16[128,512]{1,0:T(8,128)(2,1)}, u32[]{:S(2)}) copy-start(bf16[128,512]{1,0:T(8,128)(2,1)} %param.21) | copy-start | bytes 393220
  98.0 22.3 %all-to-all-start.1 = ((bf16[8,2,6272]{2,1,0:T(2,128)(2,1)}), bf16[8,2,6272]{2,1,0:T(2,128)(2,1)S(1)}, u32[]{:S(2)}, u32[]{:S(2)}) async-start(bf16[8,2,6272]{2,1,0:T(2,128)(2,1)} %reshape.413), calls=%async_computation.1 | async-start | bytes 401408 | tf_op jit(solution)/shard_map/all_to_all | solution.py:212
  101.6 109.1 %reduce-scatter.7.cloned.1.call-start = ((), (), s32[]{:S(2)}) async-start(), calls=%async_computation.12 | async-start | bytes 655360 | tf_op jit(solution)/shard_map/reduce_scatter | solution.py:283
  112.4 8.8 %copy-start.8 = (bf16[1,7,28,512]{3,2,1,0:T(8,128)(2,1)S(1)}, bf16[1,7,28,512]{3,2,1,0:T(8,128)(2,1)}, u32[]{:S(2)}) copy-start(bf16[1,7,28,512]{3,2,1,0:T(8,128)(2,1)} %param.14) | copy-start | bytes 602116
  121.8 4.0 %copy-start.18 = (bf16[1,7,28,512]{3,2,1,0:T(8,128)(2,1)S(1)}, bf16[1,7,28,512]{3,2,1,0:T(8,128)(2,1)}, u32[]{:S(2)}) copy-start(bf16[1,7,28,512]{3,2,1,0:T(8,128)(2,1)} %param.15) | copy-start | bytes 602116
  125.8 3.3 copy-start.12
  129.1 1.4 copy-start.38
  129.1 2.1 copy-start.19
  131.5 5.3 %copy-start.4 = (f32[1,7,28,512]{3,2,1,0:T(8,128)}, f32[1,7,28,512]{3,2,1,0:T(8,128)S(1)}, u32[]{:S(2)}) copy-start(f32[1,7,28,512]{3,2,1,0:T(8,128)S(1)} %fusion.67) | copy-start | bytes 1204228
  132.6 78.2 %reduce-scatter.9.cloned.1.call-start = ((), (), s32[]{:S(2)}) async-start(), calls=%async_computation.13 | async-start | bytes 2621440 | tf_op jit(solution)/shard_map/reduce_scatter | solution.py:295
  141.5 14.4 %all-to-all-start.2 = ((bf16[8,2,6272]{2,1,0:T(2,128)(2,1)}), bf16[8,2,6272]{2,1,0:T(2,128)(2,1)S(1)}, u32[]{:S(2)}, u32[]{:S(2)}) async-start(bf16[8,2,6272]{2,1,0:T(2,128)(2,1)} %reshape.415), calls=%async_computation.2 | async-start | bytes 401408 | tf_op jit(solution)/shard_map/all_to_all | solution.py:249
  147.4 74.6 %reduce-scatter.11.cloned.1.call-start = ((), (), s32[]{:S(2)}) async-start(), calls=%async_computation.14 | async-start | bytes 2621440 | tf_op jit(solution)/shard_map/reduce_scatter | solution.py:298
  150.8 101.8 %reduce-scatter.5.cloned.1.call-start = ((), (), s32[]{:S(2)}) async-start(), calls=%async_computation.11 | async-start | bytes 1966080 | tf_op jit(solution)/shard_map/reduce_scatter | solution.py:280
  160.5 3.3 copy-start.15
  163.8 3.9 %copy-start.14 = (bf16[1,1,8,4,2,49,32]{5,6,4,3,2,1,0:T(8,128)(2,1)S(1)}, bf16[1,1,8,4,2,49,32]{5,6,4,3,2,1,0:T(8,128)(2,1)}, u32[]{:S(2)}) copy-start(bf16[1,1,8,4,2,49,32]{5,6,4,3,2,1,0:T(8,128)(2,1)} %copy.160) | copy-start | bytes 602116
  169.1 2.2 copy-start.1
  171.4 3.1 copy-start.10
  172.8 1.7 copy-start.11
  205.5 1.4 copy-start.9
  205.5 1.4 copy-start.22
  205.5 1.4 copy-start.24
  205.5 1.4 copy-start.30
  206.9 2.0 copy-start.36
  208.8 43.9 %copy-start.6 = (bf16[7,28,2048]{2,1,0:T(8,128)(2,1)S(1)}, bf16[7,28,2048]{2,1,0:T(8,128)(2,1)}, u32[]{:S(2)}) copy-start(bf16[7,28,2048]{2,1,0:T(8,128)(2,1)} %get-tuple-element.86) | copy-start | bytes 2408452
  208.8 137.3 %all-reduce.10.cloned.1.call-start = ((), (), s32[]{:S(2)}) async-start(), calls=%async_computation.15 | async-start | bytes 3145728 | tf_op jit(solution)/shard_map/psum | solution.py:305
  252.7 3.1 copy-start.35
  256.8 2.3 copy-start.27
  256.8 2.3 copy-start.31
  256.8 37.6 %copy-start.5 = (f32[1,7,28,512]{3,2,1,0:T(8,128)S(1)}, f32[1,7,28,512]{3,2,1,0:T(8,128)}, u32[]{:S(2)}) copy-start(f32[1,7,28,512]{3,2,1,0:T(8,128)} %copy-done.4) | copy-start | bytes 1204228
  346.1 3.7 %copy-start.17 = (bf16[128,2048]{1,0:T(8,128)(2,1)S(1)}, bf16[128,2048]{1,0:T(8,128)(2,1)}, u32[]{:S(2)}) copy-start(bf16[128,2048]{1,0:T(8,128)(2,1)} %get-tuple-element.70) | copy-start | bytes 1572868
  346.1 4.7 %copy-start.16 = (bf16[512,512]{1,0:T(8,128)(2,1)S(1)}, bf16[512,512]{1,0:T(8,128)(2,1)}, u32[]{:S(2)}) copy-start(bf16[512,512]{1,0:T(8,128)(2,1)} %get-tuple-element.71) | copy-start | bytes 1572868
  (2 other events, 2.0 us)
Sparse Core Ops, SparseCore 0:
  10.1 22.5 all-gather.8
  34.3 22.5 all-gather.10
  58.5 22.5 all-gather.12
  132.7 22.0 reduce-scatter.6
  157.3 31.1 reduce-scatter.8
  190.8 31.1 reduce-scatter.10
  224.5 28.0 reduce-scatter.4
  256.4 89.6 all-reduce.9
